TPU v7x, 32 devices: a whole 2x2x4 slice. The times are simulated.
32 devices in a mesh: member: 4 (over y, x), slab: 8 (over z, core).
Axes of the slice: x: 2, y: 2, z: 4, core: 2. Of those that a mesh axis runs over, the one named last changes fastest.
Arguments:
- control: float32 [16, 2, 1024, 2048], P('member', None, 'slab'), may hold values from -6 to 6
- perturbation: bfloat16 [16, 2, 1024, 2048], P('member', None, 'slab'), may hold values from -6 to 6
- loc_row: float32 [2, 1024], P(None, 'slab'), may hold values from 0.2 to 2
- loc_col: float32 [2, 2048], replicated, may hold values from 0.2 to 2
- obs_tile: int32 [2048], P('slab'), may hold values from 0 to 4095, as said below
- obs_count: int32 [2048], P('slab'), may hold values from 1 to 128
- obs_value: float32 [2048, 128], P('slab'), may hold values from -12 to 12
Outputs:
- gradient: float32 [16, 2, 1024, 2048], P('member', None, 'slab')
Inputs may be any that keep to these rules, and one draw needn't show every extreme that they name: `obs_tile`: entry i names a tile of slab block i // 256 in that block's numbering, whose columns lie in column share k = (i mod 256) // (256 / 8), i.e. columns k * 2048 / 8 onward; tiles may repeat. cells 0 to obs_count - 1 of a tile are observed.
All inputs are finite; a program needn't handle non-finite values.
Results may differ from a plain program's by a relative error of at most 0.012.
Values may be sent and summed in bfloat16 or wider, within the bound.
A program may use at most 64 MiB of HBM per device.

v0:
```python
import jax
import jax.numpy as jnp
from jax import lax
from jax.sharding import PartitionSpec as P

TILE = 128


def hartley(order):
    index = jnp.arange(order, dtype=jnp.int32)
    product = index[:, None] * index[None, :] % order
    angle = 2.0 * jnp.pi * product.astype(jnp.float32) / order
    table = (jnp.cos(angle) + jnp.sin(angle)) / jnp.sqrt(jnp.float32(order))
    return table.astype(jnp.bfloat16)


def shards(control, perturbation, loc_row, loc_col, obs_tile, obs_count, obs_value):
    members, levels, rows, width = control.shape
    slabs = lax.axis_size("slab")
    height = rows * slabs
    share = width // slabs
    table_y = hartley(height)
    table_x = hartley(width)
    amplitude = loc_row[:, :, None] * loc_col[:, None, :]

    def columns_pass(block):
        product = jnp.einsum("ya,mlac->mlyc", table_y, block, preferred_element_type=jnp.float32)
        return product.astype(jnp.bfloat16)

    scaled = (control * amplitude[None]).astype(jnp.bfloat16)
    along = jnp.dot(scaled.reshape(-1, width), table_x, preferred_element_type=jnp.float32)
    along = along.astype(jnp.bfloat16).reshape(members, levels, rows, width)
    field_cols = columns_pass(
        lax.all_to_all(along, "slab", split_axis=3, concat_axis=2, tiled=True)
    )
    tile_total = levels * rows * (width // TILE)
    all_tiles = lax.all_gather(obs_tile, "slab", axis=0, tiled=True)
    per_peer = obs_tile.shape[0] // slabs
    mine = lax.axis_index("slab")
    listed = lax.dynamic_slice_in_dim(all_tiles.reshape(slabs, slabs, per_peer), mine, 1, 1)
    listed = listed.reshape(slabs, per_peer)
    per_row = width // TILE
    level = listed // (rows * per_row)
    row_in = listed // per_row % rows
    local_tile = listed % per_row - mine * (share // TILE)
    source = jnp.arange(slabs, dtype=jnp.int32)[:, None]
    flat_index = ((level * height + source * rows + row_in) * (share // TILE) + local_tile).reshape(
        -1
    )
    picked = field_cols.reshape(members, -1, TILE)[:, flat_index]
    field_obs = lax.all_to_all(picked, "slab", split_axis=1, concat_axis=1, tiled=True)
    pert_obs = perturbation.reshape(members, -1, TILE)[:, obs_tile].astype(jnp.float32)
    partial_obs = jnp.sum(pert_obs * field_obs.astype(jnp.float32), axis=0)
    cells = lax.psum(partial_obs, "member")
    resid = cells - obs_value
    observed = jnp.arange(TILE, dtype=jnp.int32)[None, :] < obs_count[:, None]
    score = jnp.where(observed, resid / jnp.sqrt(1.0 + resid * resid / 4.0), 0.0)
    adjoint_tiles = jnp.zeros((tile_total, TILE), jnp.float32).at[obs_tile].add(score)
    weighted_obs = (pert_obs * adjoint_tiles[obs_tile][None]).astype(jnp.bfloat16)
    arrived = lax.all_to_all(weighted_obs, "slab", split_axis=1, concat_axis=1, tiled=True)
    empty = jnp.zeros((members, levels * height * (share // TILE), TILE), jnp.bfloat16)
    filled = empty.at[:, flat_index].set(arrived)
    back_cols = columns_pass(filled.reshape(members, levels, height, share))
    back = lax.all_to_all(back_cols, "slab", split_axis=2, concat_axis=3, tiled=True)
    result = jnp.dot(back.reshape(-1, width), table_x, preferred_element_type=jnp.float32)
    return result.reshape(members, levels, rows, width) * amplitude[None]


def solution(mesh):
    placed = (
        P("member", None, "slab", None),
        P("member", None, "slab", None),
        P(None, "slab"),
        P(),
        P("slab"),
        P("slab"),
        P("slab", None),
    )
    return jax.shard_map(
        shards,
        mesh=mesh,
        in_specs=placed,
        out_specs=P("member", None, "slab", None),
        check_vma=False,
    )
```

profile of v0, /device:TPU:0, one launch (start us, length us, event | category | flops | bytes accessed | tf_op | source)
XLA Modules:
  0.0 563.9 jit_solution(10304791134085167966)
XLA Ops:
  6.5 68.2 %multiply_convert_fusion.9 = bf16[2048,2048]{1,0:T(8,128)(2,1)} fusion(), kind=kLoop, calls=%fused_computation.11.clone.1.clone.clone.clone.1 | loop fusion | flops 71303168 | bytes 8388608 | tf_op jit(solution)/shard_map/dot_general | solution.py:31
  74.7 0.0 copy-done.2
  74.7 0.0 copy-done.5
  74.7 0.2 broadcast_multiply_fusion
  74.9 0.0 copy-done
  74.9 1.4 multiply_convert_fusion.3
  76.4 12.6 %fusion.18 = bf16[1024,2048]{1,0:T(8,128)(2,1)} fusion(bf16[1024,2048]{1,0:T(8,128)(2,1)S(1)} %bitcast.61, bf16[2048,2048]{1,0:T(8,128)(2,1)} %multiply_convert_fusion.9), kind=kOutput, calls=%fused_computation.34 | convolution fusion | flops 8592031744 | bytes 16777216 | tf_op jit(solution)/shard_map/dot_general | solution.py:31
  89.0 11.1 %copy.24 = bf16[4,2,128,2048]{2,1,0,3:T(2,128)(2,1)} copy(bf16[4,2,128,2048]{3,2,1,0:T(8,128)(2,1)} %bitcast.62) | data formatting | bytes 8388608 | tf_op jit(solution)/shard_map/reshape | solution.py:32
  100.1 6.5 %all-to-all-start = ((bf16[4,2,128,2048]{2,1,0,3:T(2,128)(2,1)}), bf16[4,2,128,2048]{2,1,0,3:T(2,128)(2,1)}, u32[]{:S(2)}, u32[]{:S(2)}) async-start(bf16[4,2,128,2048]{2,1,0,3:T(2,128)(2,1)} %copy.24), calls=%async_computation | async-start | bytes 8388608 | tf_op jit(solution)/shard_map/all_to_all | solution.py:34
  106.6 75.3 %all-gather = s32[8,1,256]{2,1,0:T(1,128)S(1)} all-gather(s32[1,1,256]{2,1,0:T(1,128)S(1)} %bitcast.66), channel_id=1, replica_groups=mesh['member'=4,'slab'=8] {'slab'}, dimensions={0}, use_global_device_ids=true | all-gather | bytes 9216 | tf_op jit(solution)/shard_map/all_gather | solution.py:37
  181.9 0.1 reshape.231
  182.0 0.1 reshape.232
  182.1 0.1 add.140
  182.1 0.1 add.141
  182.3 18.5 %all-to-all-done = bf16[4,2,128,2048]{2,1,0,3:T(2,128)(2,1)} async-done(((bf16[4,2,128,2048]{2,1,0,3:T(2,128)(2,1)}), bf16[4,2,128,2048]{2,1,0,3:T(2,128)(2,1)}, u32[]{:S(2)}, u32[]{:S(2)}) %all-to-all-start) | async-done | bytes 4194336 | tf_op jit(solution)/shard_map/all_to_all | solution.py:34
  200.7 6.9 %copy.38 = bf16[4,2,128,8,256]{2,3,4,1,0:T(8,128)(2,1)} copy(bf16[4,2,128,8,256]{2,1,0,4,3:T(2,128)(2,1)} %bitcast.5) | data formatting | bytes 8388608 | tf_op jit(solution)/shard_map/all_to_all | solution.py:34
  207.6 7.3 %all_to_all.33 = bf16[4,2,1024,256]{2,3,1,0:T(8,128)(2,1)} reshape(bf16[4,2,8,128,256]{3,2,4,1,0:T(8,128)(2,1)} %bitcast.59) | data formatting | bytes 8388608 | tf_op jit(solution)/shard_map/all_to_all | solution.py:34
  214.9 23.3 %convert_bitcast_fusion.1 = bf16[4,2,1024,256]{2,3,1,0:T(8,128)(2,1)} fusion(bf16[4,2,1024,256]{2,3,1,0:T(8,128)(2,1)} %all_to_all.33), kind=kOutput, calls=%fused_computation.29 | convolution fusion | flops 4314890240 | bytes 8388608 | tf_op jit(solution)/shard_map/ya,mlac->mlyc/dot_general | solution.py:27
  238.2 6.2 %copy.26 = bf16[4,2,1024,256]{3,2,1,0:T(8,128)(2,1)} copy(bf16[4,2,1024,256]{2,3,1,0:T(8,128)(2,1)} %convert_bitcast_fusion.1) | data formatting | bytes 8388608 | tf_op jit(solution)/shard_map/convert_element_type | solution.py:28
  244.4 7.1 %reshape.236 = bf16[4,4096,128]{2,1,0:T(8,128)(2,1)} reshape(bf16[4,2,1024,256]{3,2,1,0:T(8,128)(2,1)} %copy.26) | data formatting | bytes 8388608 | tf_op jit(solution)/shard_map/reshape | solution.py:50
  251.5 7.6 %copy.27 = bf16[4,4096,128]{2,0,1:T(4,128)(2,1)} copy(bf16[4,4096,128]{2,1,0:T(8,128)(2,1)} %reshape.236) | data formatting | bytes 8388608 | tf_op jit(solution)/shard_map/reshape | solution.py:50
  259.1 3.8 gather_fusion.1
  262.9 6.0 %all-to-all-start.1 = ((bf16[4,256,128]{2,0,1:T(4,128)(2,1)}), bf16[4,256,128]{2,0,1:T(4,128)(2,1)S(1)}, u32[]{:S(2)}, u32[]{:S(2)}) async-start(bf16[4,256,128]{2,0,1:T(4,128)(2,1)} %bitcast.10), calls=%async_computation.1 | async-start | bytes 524288 | tf_op jit(solution)/shard_map/all_to_all | solution.py:51
  268.9 0.2 all-reduce.2.cloned.1.call-start
  269.1 7.4 %reshape.233 = bf16[4,4096,128]{2,1,0:T(8,128)(2,1)} reshape(bf16[4,2,128,2048]{3,2,1,0:T(8,128)(2,1)} %param.8) | data formatting | bytes 8388608 | tf_op jit(solution)/shard_map/reshape | solution.py:52
  276.5 7.6 %copy.23 = bf16[4,4096,128]{2,0,1:T(4,128)(2,1)} copy(bf16[4,4096,128]{2,1,0:T(8,128)(2,1)} %reshape.233) | data formatting | bytes 8388608 | tf_op jit(solution)/shard_map/reshape | solution.py:52
  284.1 3.2 gather_fusion
  287.3 0.0 all-to-all-done.1
  287.3 1.0 fusion.30
  288.4 0.0 all-reduce.2.cloned.1.call-update
  288.4 43.8 %all-reduce.2.cloned.1.call-done = f32[256,128]{1,0:T(8,128)} async-done(((f32[256,128]{1,0:T(8,128)}), f32[256,128]{1,0:T(8,128)}) %all-reduce.2.cloned.1.call-update) | async-done | bytes 131088 | tf_op jit(solution)/shard_map/psum | solution.py:54
  332.2 0.0 copy-done.1
  332.2 3.3 scatter_custom_fusion
  335.5 2.3 gather_fusion.2
  337.8 0.1 fusion.31
  337.9 14.1 %all_to_all.43 = bf16[4,256,128]{2,0,1:T(4,128)(2,1)S(1)} all-to-all(bf16[4,256,128]{2,0,1:T(4,128)(2,1)S(1)} %fusion.31), channel_id=1, replica_groups=mesh['member'=4,'slab'=8] {'slab'}, dimensions={1} | all-to-all | bytes 524288 | tf_op jit(solution)/shard_map/all_to_all | solution.py:60
  352.0 2.8 broadcast_in_dim.9
  354.9 28.1 %scatter_fusion = bf16[4,4096,128]{2,0,1:T(4,128)(2,1)} fusion(bf16[4,4096,128]{2,0,1:T(4,128)(2,1)} %broadcast_in_dim.9, s32[256]{0:T(256)S(1)} %bitcast.65, bf16[256,4,128]{2,1,0:T(4,128)(2,1)S(1)} %bitcast.63), kind=kCustom, calls=%fused_computation.4 | custom fusion | bytes 787456 | tf_op jit(solution)/shard_map/scatter | solution.py:62
  382.9 4.7 copy.28
  387.6 7.1 %reshape.237 = bf16[4,2,1024,256]{3,2,1,0:T(8,128)(2,1)} reshape(bf16[4,4096,128]{2,1,0:T(8,128)(2,1)} %copy.28) | data formatting | bytes 8388608 | tf_op jit(solution)/shard_map/reshape | solution.py:63
  394.7 23.8 %convert_bitcast_fusion = bf16[4,2,1024,256]{2,3,1,0:T(8,128)(2,1)} fusion(bf16[4,2,1024,256]{3,2,1,0:T(8,128)(2,1)} %reshape.237), kind=kOutput, calls=%fused_computation.28 | convolution fusion | flops 4314890240 | bytes 8388608 | tf_op jit(solution)/shard_map/ya,mlac->mlyc/dot_general | solution.py:27
  418.4 11.1 %copy.30 = bf16[4,2,1024,256]{3,1,0,2:T(2,128)(2,1)} copy(bf16[4,2,1024,256]{2,3,1,0:T(8,128)(2,1)} %convert_bitcast_fusion) | data formatting | bytes 8388608 | tf_op jit(solution)/shard_map/convert_element_type | solution.py:28
  429.6 4.8 all-to-all-start.3
  434.4 68.2 %fusion.75 = bf16[2048,2048,1,1]{1,0,3,2:T(8,128)(2,1)} fusion(), kind=kLoop, calls=%fused_computation.16.clone.clone.clone.1 | loop fusion | flops 71303168 | bytes 8388608 | tf_op jit(solution)/shard_map/dot_general | solution.py:65
  502.6 25.8 %all-to-all-done.3 = bf16[4,2,1024,256]{3,1,0,2:T(2,128)(2,1)} async-done(((bf16[4,2,1024,256]{3,1,0,2:T(2,128)(2,1)}), bf16[4,2,1024,256]{3,1,0,2:T(2,128)(2,1)}, u32[]{:S(2)}, u32[]{:S(2)}) %all-to-all-start.3) | async-done | bytes 4194336 | tf_op jit(solution)/shard_map/all_to_all | solution.py:64
  528.4 6.6 %copy.37 = bf16[4,2,8,128,256]{4,2,3,1,0:T(8,128)(2,1)} copy(bf16[4,2,8,128,256]{4,1,0,3,2:T(2,128)(2,1)} %bitcast.13) | data formatting | bytes 8388608 | tf_op jit(solution)/shard_map/all_to_all | solution.py:64
  534.9 7.4 %dot_general.17 = bf16[4,2,128,2048]{3,2,1,0:T(8,128)(2,1)} reshape(bf16[4,2,128,8,256]{4,3,2,1,0:T(8,128)(2,1)} %bitcast.60) | data formatting | bytes 8388608 | tf_op jit(solution)/shard_map/dot_general | solution.py:65
  542.3 14.5 %fusion.9 = f32[4,2,128,2048]{3,2,1,0:T(8,128)} fusion(bf16[4,2,128,2048]{3,2,1,0:T(8,128)(2,1)} %dot_general.17, f32[2,128,2048]{2,1,0:T(8,128)S(1)} %broadcast_multiply_fusion, bf16[2048,2048,1,1]{1,0,3,2:T(8,128)(2,1)} %fusion.75), kind=kOutput, calls=%fused_computation.22 | convolution fusion | flops 8592031744 | bytes 23068672 | tf_op jit(solution)/shard_map/dot_general | solution.py:65
  (15 shorter events, 0.1 us)
Async XLA Ops:
  6.5 68.2 %copy-start.2 = (f32[2,2048]{1,0:T(2,128)S(1)}, f32[2,2048]{1,0:T(2,128)}, u32[]{:S(2)}) copy-start(f32[2,2048]{1,0:T(2,128)} %param.10) | copy-start | bytes 49156
  6.5 68.2 %copy-start.5 = (f32[2,128]{1,0:T(2,128)S(1)}, f32[2,128]{1,0:T(2,128)}, u32[]{:S(2)}) copy-start(f32[2,128]{1,0:T(2,128)} %param.9) | copy-start | bytes 3076
  6.5 68.4 %copy-start = (f32[4,2,128,2048]{3,2,1,0:T(8,128)S(1)}, f32[4,2,128,2048]{3,2,1,0:T(8,128)}, u32[]{:S(2)}) copy-start(f32[4,2,128,2048]{3,2,1,0:T(8,128)} %param.7) | copy-start | bytes 25165828
  100.1 6.5 %copy-start.3 = (s32[256]{0:T(256)S(1)}, s32[256]{0:T(256)}, u32[]{:S(2)}) copy-start(s32[256]{0:T(256)} %param.11) | copy-start | bytes 3076
  100.1 100.6 %all-to-all-start = ((bf16[4,2,128,2048]{2,1,0,3:T(2,128)(2,1)}), bf16[4,2,128,2048]{2,1,0,3:T(2,128)(2,1)}, u32[]{:S(2)}, u32[]{:S(2)}) async-start(bf16[4,2,128,2048]{2,1,0,3:T(2,128)(2,1)} %copy.24), calls=%async_computation | async-start | bytes 8388608 | tf_op jit(solution)/shard_map/all_to_all | solution.py:34
  262.9 24.4 %all-to-all-start.1 = ((bf16[4,256,128]{2,0,1:T(4,128)(2,1)}), bf16[4,256,128]{2,0,1:T(4,128)(2,1)S(1)}, u32[]{:S(2)}, u32[]{:S(2)}) async-start(bf16[4,256,128]{2,0,1:T(4,128)(2,1)} %bitcast.10), calls=%async_computation.1 | async-start | bytes 524288 | tf_op jit(solution)/shard_map/all_to_all | solution.py:51
  268.9 63.3 %all-reduce.2.cloned.1.call-start = ((), (), s32[]{:S(2)}) async-start(), calls=%async_computation.4 | async-start | bytes 262144 | tf_op jit(solution)/shard_map/psum | solution.py:54
  276.5 55.7 %copy-start.1 = (f32[256,128]{1,0:T(8,128)S(1)}, f32[256,128]{1,0:T(8,128)}, u32[]{:S(2)}) copy-start(f32[256,128]{1,0:T(8,128)} %param.13) | copy-start | bytes 393220
  276.5 55.7 %copy-start.4 = (s32[256]{0:T(256)S(1)}, s32[256]{0:T(256)}, u32[]{:S(2)}) copy-start(s32[256]{0:T(256)} %param.12) | copy-start | bytes 3076
  429.6 98.8 %all-to-all-start.3 = ((bf16[4,2,1024,256]{3,1,0,2:T(2,128)(2,1)}), bf16[4,2,1024,256]{3,1,0,2:T(2,128)(2,1)}, u32[]{:S(2)}, u32[]{:S(2)}) async-start(bf16[4,2,1024,256]{3,1,0,2:T(2,128)(2,1)} %copy.30), calls=%async_computation.3 | async-start | bytes 8388608 | tf_op jit(solution)/shard_map/all_to_all | solution.py:64
Sparse Core Ops, SparseCore 0:
  288.5 43.6 all-reduce.1
where the time goes:
time: 572 us; the launch traced here: 564 us
  other arithmetic  142 us (25%)
  local copies, waits for them, and re-layouts  139 us (24%)
  blocking collectives  89.4 us (16%)
  waiting for transfers between devices  88.1 us (15%)
  matrix products  74.1 us (13%)
  starting transfers between devices  17.5 us (3%)
  between operations  13.7 us (2%)
    all_gather x1, blocking collectives, shards(): all_tiles = lax.all_gather(obs_tile, 'slab', axis=0, tiled=True)  75.3 us
    dot_general x1, other arithmetic, shards(): jnp.dot(back.reshape(-1, width), table_x, preferred_element_type=jnp.floa...  68.2 us
    dot_general x1, other arithmetic, shards(): jnp.dot(scaled.reshape(-1, width), table_x, preferred_element_type=jnp.fl...  68.2 us
    dot_general x2, matrix products, columns_pass(): jnp.einsum('ya,mlac->mlyc', table_y, block, preferred_element_type=jnp.fl...  47.1 us
    psum x1, waiting for transfers between devices, shards(): cells = lax.psum(partial_obs, 'member')  43.8 us
    scatter x2, local copies, waits for them, and re-layouts, shards(): filled = empty.at[:, flat_index].set(arrived)  32.7 us
    all_to_all x1, waiting for transfers between devices, shards(): lax.all_to_all(back_cols, 'slab', split_axis=2, concat_axis=3, tiled=True)  25.8 us
    all_to_all x1, waiting for transfers between devices, shards(): lax.all_to_all(along, 'slab', split_axis=3, concat_axis=2, tiled=True)  18.5 us
  transfers between devices with their start and end apart: 4, of which 3 were waited for; matrix products, arithmetic and copies ran while one was open for 15% of the time, Pallas kernels for 0%

commit v1 on v0

--- a/solution.py
+++ b/solution.py
@@ -51,7 +51,11 @@
     field_obs = lax.all_to_all(picked, "slab", split_axis=1, concat_axis=1, tiled=True)
     pert_obs = perturbation.reshape(members, -1, TILE)[:, obs_tile].astype(jnp.float32)
     partial_obs = jnp.sum(pert_obs * field_obs.astype(jnp.float32), axis=0)
-    cells = lax.psum(partial_obs, "member")
+    peers = lax.axis_size("member")
+    cells, far = (partial_obs, 1)
+    while far < peers:
+        cells = cells + lax.ppermute(cells, "member", [(i, i ^ far) for i in range(peers)])
+        far = 2 * far
     resid = cells - obs_value
     observed = jnp.arange(TILE, dtype=jnp.int32)[None, :] < obs_count[:, None]
     score = jnp.where(observed, resid / jnp.sqrt(1.0 + resid * resid / 4.0), 0.0)

time: 572 us -> 525 us (0.918)
  waiting for transfers between devices: 88.1 us -> 52.2 us
  between operations: 13.7 us -> 0.34 us
    psum x1 -> x0, waiting for transfers between devices: 43.8 us -> none  [shards(): cells = lax.psum(partial_obs, 'member')]
    ppermute x0 -> x2, waiting for transfers between devices: none -> 7.93 us  [shards(): lax.ppermute(cells, 'member', [(i, i ^ far) for i in range(peers)])]
  transfers between devices with their start and end apart: 4 -> 5, of which waited for: 3 -> 4; matrix products, arithmetic and copies ran while one was open for 15% -> 17% of each run, Pallas kernels for 0% -> 0%
where the time goes in v1:
time: 525 us; the launch traced here: 517 us
  other arithmetic  141 us (27%)
  local copies, waits for them, and re-layouts  139 us (26%)
  blocking collectives  89.4 us (17%)
  matrix products  74.1 us (14%)
  waiting for transfers between devices  52.2 us (10%)
  starting transfers between devices  20.7 us (4%)
    all_gather x1, blocking collectives, shards(): all_tiles = lax.all_gather(obs_tile, 'slab', axis=0, tiled=True)  75.3 us
    dot_general x1, other arithmetic, shards(): jnp.dot(back.reshape(-1, width), table_x, preferred_element_type=jnp.floa...  68.2 us
    dot_general x1, other arithmetic, shards(): jnp.dot(scaled.reshape(-1, width), table_x, preferred_element_type=jnp.fl...  68.2 us
    dot_general x2, matrix products, columns_pass(): jnp.einsum('ya,mlac->mlyc', table_y, block, preferred_element_type=jnp.fl...  47 us
    scatter x2, local copies, waits for them, and re-layouts, shards(): filled = empty.at[:, flat_index].set(arrived)  32.7 us
    all_to_all x1, waiting for transfers between devices, shards(): lax.all_to_all(back_cols, 'slab', split_axis=2, concat_axis=3, tiled=True)  25.8 us
    all_to_all x1, waiting for transfers between devices, shards(): lax.all_to_all(along, 'slab', split_axis=3, concat_axis=2, tiled=True)  18.5 us
    convert_element_type x2, local copies, waits for them, and re-layouts, columns_pass(): return product.astype(jnp.bfloat16)  17.4 us
  transfers between devices with their start and end apart: 5, of which 4 were waited for; matrix products, arithmetic and copies ran while one was open for 17% of the time, Pallas kernels for 0%

profile of v1, /device:TPU:0, one launch (start us, length us, event | category | flops | bytes accessed | tf_op | source)
XLA Modules:
  0.0 516.8 jit_solution(6150510926545033937)
XLA Ops:
  0.0 68.2 %multiply_convert_fusion.9 = bf16[2048,2048]{1,0:T(8,128)(2,1)} fusion(), kind=kLoop, calls=%fused_computation.11.clone.1.clone.clone.clone.1 | loop fusion | flops 71303168 | bytes 8388608 | tf_op jit(solution)/shard_map/dot_general | solution.py:31
  68.2 0.0 copy-done.4
  68.2 0.2 broadcast_multiply_fusion
  68.4 1.4 multiply_convert_fusion.3
  69.8 12.6 %fusion.18 = bf16[1024,2048]{1,0:T(8,128)(2,1)} fusion(bf16[1024,2048]{1,0:T(8,128)(2,1)S(1)} %bitcast.61, bf16[2048,2048]{1,0:T(8,128)(2,1)} %multiply_convert_fusion.9), kind=kOutput, calls=%fused_computation.34 | convolution fusion | flops 8592031744 | bytes 16777216 | tf_op jit(solution)/shard_map/dot_general | solution.py:31
  82.4 11.1 %copy.24 = bf16[4,2,128,2048]{2,1,0,3:T(2,128)(2,1)} copy(bf16[4,2,128,2048]{3,2,1,0:T(8,128)(2,1)} %bitcast.62) | data formatting | bytes 8388608 | tf_op jit(solution)/shard_map/reshape | solution.py:32
  93.6 6.5 %all-to-all-start = ((bf16[4,2,128,2048]{2,1,0,3:T(2,128)(2,1)}), bf16[4,2,128,2048]{2,1,0,3:T(2,128)(2,1)}, u32[]{:S(2)}, u32[]{:S(2)}) async-start(bf16[4,2,128,2048]{2,1,0,3:T(2,128)(2,1)} %copy.24), calls=%async_computation | async-start | bytes 8388608 | tf_op jit(solution)/shard_map/all_to_all | solution.py:34
  100.0 0.0 copy-done.3
  100.1 75.3 %all-gather = s32[8,1,256]{2,1,0:T(1,128)S(1)} all-gather(s32[1,1,256]{2,1,0:T(1,128)S(1)} %bitcast.66), channel_id=1, replica_groups=mesh['member'=4,'slab'=8] {'slab'}, dimensions={0}, use_global_device_ids=true | all-gather | bytes 9216 | tf_op jit(solution)/shard_map/all_gather | solution.py:37
  175.3 0.1 reshape.231
  175.4 0.1 reshape.232
  175.5 0.1 add.144
  175.6 0.1 add.145
  175.7 18.5 %all-to-all-done = bf16[4,2,128,2048]{2,1,0,3:T(2,128)(2,1)} async-done(((bf16[4,2,128,2048]{2,1,0,3:T(2,128)(2,1)}), bf16[4,2,128,2048]{2,1,0,3:T(2,128)(2,1)}, u32[]{:S(2)}, u32[]{:S(2)}) %all-to-all-start) | async-done | bytes 4194336 | tf_op jit(solution)/shard_map/all_to_all | solution.py:34
  194.2 6.9 %copy.38 = bf16[4,2,128,8,256]{2,3,4,1,0:T(8,128)(2,1)} copy(bf16[4,2,128,8,256]{2,1,0,4,3:T(2,128)(2,1)} %bitcast.5) | data formatting | bytes 8388608 | tf_op jit(solution)/shard_map/all_to_all | solution.py:34
  201.1 7.3 %all_to_all.33 = bf16[4,2,1024,256]{2,3,1,0:T(8,128)(2,1)} reshape(bf16[4,2,8,128,256]{3,2,4,1,0:T(8,128)(2,1)} %bitcast.59) | data formatting | bytes 8388608 | tf_op jit(solution)/shard_map/all_to_all | solution.py:34
  208.4 23.3 %convert_bitcast_fusion.1 = bf16[4,2,1024,256]{2,3,1,0:T(8,128)(2,1)} fusion(bf16[4,2,1024,256]{2,3,1,0:T(8,128)(2,1)} %all_to_all.33), kind=kOutput, calls=%fused_computation.29 | convolution fusion | flops 4314890240 | bytes 8388608 | tf_op jit(solution)/shard_map/ya,mlac->mlyc/dot_general | solution.py:27
  231.7 6.2 %copy.26 = bf16[4,2,1024,256]{3,2,1,0:T(8,128)(2,1)} copy(bf16[4,2,1024,256]{2,3,1,0:T(8,128)(2,1)} %convert_bitcast_fusion.1) | data formatting | bytes 8388608 | tf_op jit(solution)/shard_map/convert_element_type | solution.py:28
  237.9 7.1 %reshape.236 = bf16[4,4096,128]{2,1,0:T(8,128)(2,1)} reshape(bf16[4,2,1024,256]{3,2,1,0:T(8,128)(2,1)} %copy.26) | data formatting | bytes 8388608 | tf_op jit(solution)/shard_map/reshape | solution.py:50
  245.0 7.6 %copy.27 = bf16[4,4096,128]{2,0,1:T(4,128)(2,1)} copy(bf16[4,4096,128]{2,1,0:T(8,128)(2,1)} %reshape.236) | data formatting | bytes 8388608 | tf_op jit(solution)/shard_map/reshape | solution.py:50
  252.6 3.9 gather_fusion.1
  256.4 6.2 %all-to-all-start.1 = ((bf16[4,256,128]{2,0,1:T(4,128)(2,1)}), bf16[4,256,128]{2,0,1:T(4,128)(2,1)S(1)}, u32[]{:S(2)}, u32[]{:S(2)}) async-start(bf16[4,256,128]{2,0,1:T(4,128)(2,1)} %bitcast.10), calls=%async_computation.1 | async-start | bytes 524288 | tf_op jit(solution)/shard_map/all_to_all | solution.py:51
  262.6 7.4 %reshape.233 = bf16[4,4096,128]{2,1,0:T(8,128)(2,1)} reshape(bf16[4,2,128,2048]{3,2,1,0:T(8,128)(2,1)} %param.8) | data formatting | bytes 8388608 | tf_op jit(solution)/shard_map/reshape | solution.py:52
  270.0 7.6 %copy.23 = bf16[4,4096,128]{2,0,1:T(4,128)(2,1)} copy(bf16[4,4096,128]{2,1,0:T(8,128)(2,1)} %reshape.233) | data formatting | bytes 8388608 | tf_op jit(solution)/shard_map/reshape | solution.py:52
  277.6 3.2 gather_fusion
  280.8 0.0 all-to-all-done.1
  280.8 0.4 fusion.30
  281.2 1.6 collective-permute-start
  282.8 4.4 collective-permute-done
  287.2 1.6 collective-permute-start.1
  288.8 3.5 collective-permute-done.1
  292.3 0.0 copy-done.1
  292.3 2.9 scatter_custom_fusion
  295.2 2.3 gather_fusion.2
  297.5 0.1 fusion.31
  297.7 14.1 %all_to_all.43 = bf16[4,256,128]{2,0,1:T(4,128)(2,1)S(1)} all-to-all(bf16[4,256,128]{2,0,1:T(4,128)(2,1)S(1)} %fusion.31), channel_id=1, replica_groups=mesh['member'=4,'slab'=8] {'slab'}, dimensions={1} | all-to-all | bytes 524288 | tf_op jit(solution)/shard_map/all_to_all | solution.py:64
  311.8 2.8 broadcast_in_dim.9
  314.6 28.1 %scatter_fusion = bf16[4,4096,128]{2,0,1:T(4,128)(2,1)} fusion(bf16[4,4096,128]{2,0,1:T(4,128)(2,1)} %broadcast_in_dim.9, s32[256]{0:T(256)S(1)} %bitcast.65, bf16[256,4,128]{2,1,0:T(4,128)(2,1)S(1)} %bitcast.63), kind=kCustom, calls=%fused_computation.4 | custom fusion | bytes 787456 | tf_op jit(solution)/shard_map/scatter | solution.py:66
  342.7 4.7 copy.28
  347.4 7.1 %reshape.237 = bf16[4,2,1024,256]{3,2,1,0:T(8,128)(2,1)} reshape(bf16[4,4096,128]{2,1,0:T(8,128)(2,1)} %copy.28) | data formatting | bytes 8388608 | tf_op jit(solution)/shard_map/reshape | solution.py:67
  354.4 23.8 %convert_bitcast_fusion = bf16[4,2,1024,256]{2,3,1,0:T(8,128)(2,1)} fusion(bf16[4,2,1024,256]{3,2,1,0:T(8,128)(2,1)} %reshape.237), kind=kOutput, calls=%fused_computation.28 | convolution fusion | flops 4314890240 | bytes 8388608 | tf_op jit(solution)/shard_map/ya,mlac->mlyc/dot_general | solution.py:27
  378.2 11.1 %copy.30 = bf16[4,2,1024,256]{3,1,0,2:T(2,128)(2,1)} copy(bf16[4,2,1024,256]{2,3,1,0:T(8,128)(2,1)} %convert_bitcast_fusion) | data formatting | bytes 8388608 | tf_op jit(solution)/shard_map/convert_element_type | solution.py:28
  389.3 4.8 all-to-all-start.3
  394.2 68.2 %fusion.76 = bf16[2048,2048,1,1]{1,0,3,2:T(8,128)(2,1)} fusion(), kind=kLoop, calls=%fused_computation.16.clone.clone.clone.1 | loop fusion | flops 71303168 | bytes 8388608 | tf_op jit(solution)/shard_map/dot_general | solution.py:69
  462.3 25.8 %all-to-all-done.3 = bf16[4,2,1024,256]{3,1,0,2:T(2,128)(2,1)} async-done(((bf16[4,2,1024,256]{3,1,0,2:T(2,128)(2,1)}), bf16[4,2,1024,256]{3,1,0,2:T(2,128)(2,1)}, u32[]{:S(2)}, u32[]{:S(2)}) %all-to-all-start.3) | async-done | bytes 4194336 | tf_op jit(solution)/shard_map/all_to_all | solution.py:68
  488.1 6.6 %copy.37 = bf16[4,2,8,128,256]{4,2,3,1,0:T(8,128)(2,1)} copy(bf16[4,2,8,128,256]{4,1,0,3,2:T(2,128)(2,1)} %bitcast.13) | data formatting | bytes 8388608 | tf_op jit(solution)/shard_map/all_to_all | solution.py:68
  494.7 7.4 %dot_general.17 = bf16[4,2,128,2048]{3,2,1,0:T(8,128)(2,1)} reshape(bf16[4,2,128,8,256]{4,3,2,1,0:T(8,128)(2,1)} %bitcast.60) | data formatting | bytes 8388608 | tf_op jit(solution)/shard_map/dot_general | solution.py:69
  502.1 14.5 %fusion.9 = f32[4,2,128,2048]{3,2,1,0:T(8,128)} fusion(bf16[4,2,128,2048]{3,2,1,0:T(8,128)(2,1)} %dot_general.17, f32[2,128,2048]{2,1,0:T(8,128)S(1)} %broadcast_multiply_fusion, bf16[2048,2048,1,1]{1,0,3,2:T(8,128)(2,1)} %fusion.76), kind=kOutput, calls=%fused_computation.22 | convolution fusion | flops 8592031744 | bytes 23068672 | tf_op jit(solution)/shard_map/dot_general | solution.py:69
  (17 shorter events, 0.1 us)
Async XLA Ops:
  0.0 68.2 %copy-start.2 = (f32[2,2048]{1,0:T(2,128)S(1)}, f32[2,2048]{1,0:T(2,128)}, u32[]{:S(2)}) copy-start(f32[2,2048]{1,0:T(2,128)} %param.10) | copy-start | bytes 49156
  0.0 68.2 %copy-start.4 = (f32[2,128]{1,0:T(2,128)S(1)}, f32[2,128]{1,0:T(2,128)}, u32[]{:S(2)}) copy-start(f32[2,128]{1,0:T(2,128)} %param.9) | copy-start | bytes 3076
  0.0 68.4 %copy-start = (f32[4,2,128,2048]{3,2,1,0:T(8,128)S(1)}, f32[4,2,128,2048]{3,2,1,0:T(8,128)}, u32[]{:S(2)}) copy-start(f32[4,2,128,2048]{3,2,1,0:T(8,128)} %param.7) | copy-start | bytes 25165828
  93.6 6.5 %copy-start.3 = (s32[256]{0:T(256)S(1)}, s32[256]{0:T(256)}, u32[]{:S(2)}) copy-start(s32[256]{0:T(256)} %param.11) | copy-start | bytes 3076
  93.6 100.6 %all-to-all-start = ((bf16[4,2,128,2048]{2,1,0,3:T(2,128)(2,1)}), bf16[4,2,128,2048]{2,1,0,3:T(2,128)(2,1)}, u32[]{:S(2)}, u32[]{:S(2)}) async-start(bf16[4,2,128,2048]{2,1,0,3:T(2,128)(2,1)} %copy.24), calls=%async_computation | async-start | bytes 8388608 | tf_op jit(solution)/shard_map/all_to_all | solution.py:34
  256.4 24.4 %all-to-all-start.1 = ((bf16[4,256,128]{2,0,1:T(4,128)(2,1)}), bf16[4,256,128]{2,0,1:T(4,128)(2,1)S(1)}, u32[]{:S(2)}, u32[]{:S(2)}) async-start(bf16[4,256,128]{2,0,1:T(4,128)(2,1)} %bitcast.10), calls=%async_computation.1 | async-start | bytes 524288 | tf_op jit(solution)/shard_map/all_to_all | solution.py:51
  270.0 22.3 %copy-start.1 = (f32[256,128]{1,0:T(8,128)S(1)}, f32[256,128]{1,0:T(8,128)}, u32[]{:S(2)}) copy-start(f32[256,128]{1,0:T(8,128)} %param.13) | copy-start | bytes 393220
  270.0 22.3 %copy-start.5 = (s32[256]{0:T(256)S(1)}, s32[256]{0:T(256)}, u32[]{:S(2)}) copy-start(s32[256]{0:T(256)} %param.12) | copy-start | bytes 3076
  281.2 6.0 %collective-permute-start = (f32[256,128]{1,0:T(8,128)S(1)}, f32[256,128]{1,0:T(8,128)S(1)}, u32[]{:S(2)}, u32[]{:S(2)}) collective-permute-start(f32[256,128]{1,0:T(8,128)S(1)} %fusion.30), channel_id=1, source_target_pairs={{0,8},{8,0},{16,24},{24,16},{1,9},{9,1},{17,25},{25,17},{2,10},{10... | collective-permute-start | bytes 393224 | tf_op jit(solution)/shard_map/ppermute | solution.py:57
  287.2 5.1 collective-permute-start.1
  389.3 98.8 %all-to-all-start.3 = ((bf16[4,2,1024,256]{3,1,0,2:T(2,128)(2,1)}), bf16[4,2,1024,256]{3,1,0,2:T(2,128)(2,1)}, u32[]{:S(2)}, u32[]{:S(2)}) async-start(bf16[4,2,1024,256]{3,1,0,2:T(2,128)(2,1)} %copy.30), calls=%async_computation.3 | async-start | bytes 8388608 | tf_op jit(solution)/shard_map/all_to_all | solution.py:68
